TPU v7x, 128 devices: a whole 4x4x4 slice. The times are simulated.
128 devices in a mesh: row: 8 (over z_hi, x), blk: 16 (over z_lo, y, core).
Axes of the slice: x: 4, y: 4, z: 4 (z_hi: 2, z_lo: 2; z = z_hi * 2 + z_lo), core: 2. Of those that a mesh axis runs over, the one named last changes fastest.
Arguments:
- spike_counts: int32 [16384, 2048], P(('row', 'blk')), may hold values from 0 to 23, as said below
- kernel_taps: int32 [16], replicated, may hold values from 1 to 8
- lag_bins: int32 [2], replicated, may hold values from 1 to 32, as said below
Outputs:
- correlogram: bfloat16 [2, 16384, 8, 2048], P(None, 'row', None, 'blk')
Inputs may be any that keep to these rules, and one draw needn't show every extreme that they name: `spike_counts`: neurons fire at different rates and share a common drive. `lag_bins`: the second lag equals 32; the first lies between 1 and 31.
All inputs are finite; a program needn't handle non-finite values.
Results may differ from a plain program's by a relative error of at most 0.0034.
Values may be sent and summed in bfloat16 or wider, within the bound.
A program may use at most 128 MiB of HBM per device.

v0:
```python
import jax
import jax.numpy as jnp
from jax import lax
from jax.sharding import PartitionSpec as P

NEURONS = 16384
BINS = 2048
TAPS = 16


def smoothed(spike_counts, kernel_taps):
    counts = spike_counts.astype(jnp.float32)
    weights = kernel_taps.astype(jnp.float32) / jnp.sum(kernel_taps.astype(jnp.float32))
    padded = jnp.pad(counts, ((0, 0), (TAPS - 1, 0)))
    result = jnp.zeros_like(counts)
    for delay in range(TAPS):
        result = result + weights[delay] * padded[:, TAPS - 1 - delay : TAPS - 1 - delay + BINS]
    return result


def later_bins(data, lag):
    padded = jnp.pad(data, ((0, 0), (0, BINS)))
    return lax.dynamic_slice_in_dim(padded, lag, BINS, 1)


def shards(spike_counts, kernel_taps, lag_bins):
    smooth = smoothed(spike_counts, kernel_taps)
    centred = smooth - jnp.mean(smooth, axis=1, keepdims=True)
    totals = lax.psum(jnp.sum(centred, axis=0), ("row", "blk"))
    residual_part = centred - (totals / NEURONS)[None, :]
    zscored = (
        residual_part
        * lax.rsqrt(jnp.mean(residual_part * residual_part, axis=1, keepdims=True) + 1e-05)
    ).astype(jnp.bfloat16)
    span_rows = zscored.shape[0]
    groups = lax.axis_size("row")
    columns = lax.all_gather(zscored, "row", axis=0, tiled=True)
    stacked = jnp.concatenate(
        [later_bins(columns, lag_bins[0]), later_bins(columns, lag_bins[1])], axis=0
    )
    piece = lax.all_gather(zscored, "blk", axis=0, tiled=True)
    product = jnp.dot(piece, stacked.T, preferred_element_type=jnp.float32) / BINS
    product = product.reshape(piece.shape[0], 2, groups, span_rows)
    return jnp.transpose(product, (1, 0, 2, 3)).astype(jnp.bfloat16)


def solution(mesh):
    placed = (P(("row", "blk"), None), P(), P())
    return jax.shard_map(
        shards, mesh=mesh, in_specs=placed, out_specs=P(None, "row", None, "blk"), check_vma=False
    )
```

profile of v0, /device:TPU:1, one launch (start us, length us, event | category | flops | bytes accessed | tf_op | source)
XLA Modules:
  0.0 258.9 jit_solution(15566849793997691235)
XLA Ops:
  6.5 0.0 copy-start
  6.5 0.0 all-gather.5.cloned.1.call-start
  6.5 1.3 convert_reduce_fusion
  7.8 1.3 convert_divide_fusion
  9.1 0.7 fusion.8
  9.8 1.3 convert_element_type.25
  11.2 14.1 %fusion.6 = (f32[128]{0:T(128)S(1)}, f32[128,2048]{1,0:T(8,128)S(1)}) fusion(f32[]{:T(128)} %bitcast.15, f32[]{:T(128)} %bitcast.14, f32[]{:T(128)} %bitcast.13, f32[]{:T(128)} %bitcast.12, f32[]{:T(128)} %bitcast.11, f32[]{:T(128)} %bitcast.10, f32[]{:T(128)} %bitcast.9, f32[]{:T(128)} %bitcast.8, f32[]{:T(128)} %bitcast.7, f32[]{:T(128)} %bitcast.6, ...), kind=kLoop, calls=%fused_computation.19 | loop fusion | flops 8388480 | bytes 2097728 | tf_op jit(solution)/shard_map/reduce_sum | solution.py:28
  25.3 0.2 subtract_reduce_fusion
  25.5 68.7 %psum.7 = f32[2048]{0:T(1024)S(1)} all-reduce(f32[2048]{0:T(1024)S(1)} %subtract_reduce_fusion), channel_id=1, replica_groups=mesh['row'=8,'blk'=16] {'row','blk'}, use_global_device_ids=true, to_apply=%region_3.4 | all-reduce | flops 2048 | bytes 16384 | tf_op jit(solution)/shard_map/psum | solution.py:29
  94.2 0.3 multiply_reduce_fusion
  94.5 1.0 multiply_convert_fusion.1
  95.5 0.0 all-gather.5.cloned.1.call-update
  95.6 0.2 all-gather.3.cloned.1.call-start
  95.8 0.5 all-gather.3.cloned.1.call-update
  96.3 0.0 copy-done
  96.3 0.6 fusion.7
  100.7 62.5 %all-gather.5.cloned.1.call-done = bf16[1024,2048]{1,0:T(8,128)(2,1)} async-done(((bf16[128,2048]{1,0:T(8,128)(2,1)}), bf16[1024,2048]{1,0:T(8,128)(2,1)}) %all-gather.5.cloned.1.call-update) | async-done | bytes 4194320 | tf_op jit(solution)/shard_map/all_gather | solution.py:37
  163.2 10.0 %pad_dynamic-slice_fusion.1 = (bf16[1024,2048]{1,0:T(8,128)(2,1)}, bf16[1024,2048]{1,0:T(8,128)(2,1)}) fusion(s32[]{:T(128)S(6)} %select_n.6, bf16[1024,2048]{1,0:T(8,128)(2,1)} %all-gather.5.cloned.1.call-done, s32[]{:T(128)S(6)} %select_n.7), kind=kLoop, calls=%fused_computation.2 | loop fusion | bytes 12582920 | tf_op jit(solution)/shard_map/dynamic_slice | solution.py:23
  173.2 42.5 %all-gather.3.cloned.1.call-done = bf16[2048,2048]{1,0:T(8,128)(2,1)} async-done(((bf16[128,2048]{1,0:T(8,128)(2,1)}), bf16[2048,2048]{1,0:T(8,128)(2,1)}) %all-gather.3.cloned.1.call-update) | async-done | bytes 8388624 | tf_op jit(solution)/shard_map/all_gather | solution.py:41
  215.7 23.8 %multiply_convert_fusion = bf16[2048,2048]{0,1:T(8,128)(2,1)} fusion(bf16[2048,2048]{1,0:T(8,128)(2,1)} %all-gather.3.cloned.1.call-done, bf16[1024,2048]{1,0:T(8,128)(2,1)} %get-tuple-element.8, bf16[1024,2048]{1,0:T(8,128)(2,1)} %get-tuple-element.7), kind=kOutput, calls=%fused_computation | convolution fusion | flops 17205035008 | bytes 25165824 | tf_op jit(solution)/shard_map/dot_general | solution.py:42
  239.5 12.6 %copy.4 = bf16[2048,2,8,128]{3,2,0,1:T(8,128)(2,1)} copy(bf16[2048,2,8,128]{0,3,2,1:T(8,128)(2,1)} %bitcast.21) | data formatting | bytes 16777216 | tf_op jit(solution)/shard_map/convert_element_type | solution.py:44
  (3 shorter events, 0.0 us)
Async XLA Ops:
  6.5 89.8 %copy-start = (s32[2]{0:T(128)S(1)}, s32[2]{0:T(128)}, u32[]{:S(2)}) copy-start(s32[2]{0:T(128)} %param.5) | copy-start | bytes 28
  6.5 156.7 %all-gather.5.cloned.1.call-start = ((), (), s32[]{:S(2)}) async-start(), calls=%async_computation.1 | async-start | bytes 4718592 | tf_op jit(solution)/shard_map/all_gather | solution.py:37
  95.6 120.2 %all-gather.3.cloned.1.call-start = ((), (), s32[]{:S(2)}) async-start(), calls=%async_computation | async-start | bytes 8912896 | tf_op jit(solution)/shard_map/all_gather | solution.py:41
Sparse Core Ops, SparseCore 0:
  95.7 67.5 all-gather.4
  165.0 50.7 all-gather.2
where the time goes:
time: 260 us; the launch traced here: 259 us
  waiting for transfers between devices  106 us (41%)
  blocking collectives  68.7 us (26%)
  local copies, waits for them, and re-layouts  23.9 us (9%)
  matrix products  23.8 us (9%)
  other arithmetic  19.5 us (8%)
  between operations  17.2 us (7%)
    psum x1, blocking collectives, shards(): totals = lax.psum(jnp.sum(centred, axis=0), ('row', 'blk'))  68.7 us
    all_gather x1, waiting for transfers between devices, shards(): columns = lax.all_gather(zscored, 'row', axis=0, tiled=True)  62.5 us
    all_gather x1, waiting for transfers between devices, shards(): piece = lax.all_gather(zscored, 'blk', axis=0, tiled=True)  42.5 us
    dot_general x1, matrix products, shards(): jnp.dot(piece, stacked.T, preferred_element_type=jnp.float32) / BINS  23.8 us
    reduce_sum x1, other arithmetic, shards(): centred = smooth - jnp.mean(smooth, axis=1, keepdims=True)  14.1 us
    convert_element_type x1, local copies, waits for them, and re-layouts, shards(): return jnp.transpose(product, (1, 0, 2, 3)).astype(jnp.bfloat16)  12.6 us
    dynamic_slice x1, local copies, waits for them, and re-layouts, later_bins(): return lax.dynamic_slice_in_dim(padded, lag, BINS, 1)  9.97 us
  transfers between devices with their start and end apart: 2, of which 2 were waited for; matrix products, arithmetic and copies ran while one was open for 4% of the time, Pallas kernels for 0%

commit v1 on v0

v1 whole, which is shorter than its diff:
```python
import functools

import jax
import jax.numpy as jnp
from jax import lax
from jax.experimental import pallas as pl
from jax.experimental.pallas import tpu as pltpu
from jax.sharding import PartitionSpec as P

NEURONS = 16384
BINS = 2048
TAPS = 16
LAGMAX = 32
MESH = pl.DeviceIdType.MESH
f32 = jnp.float32
bf16 = jnp.bfloat16

ROWS = 128
HALF = ROWS // 2
PAD = 128
CH = 256
NCH = BINS // CH
WIN = CH + PAD

O, XM, XP, X2, PZ, YM, YP, Y2, QZ = range(9)
S_O, S_Z, S_M, S_P, S_2, S_Z2, S_ZM, S_ZP = range(8)


def gather_kernel(taps_ref, lag_ref, counts_ref, acc_ref,
                  raw, bbuf, wz, ws, ft, fr, popt, popr, wrow, wcol, own_sum, part_sum, got1, got2,
                  snd1, rcv1, snd2, rcv2, ssem, rsem):
    row = lax.axis_index("row")
    blk = lax.axis_index("blk")
    zh, x = row // 4, row % 4
    zl, y, c = blk // 8, (blk // 2) % 4, blk % 2

    def at(zh_, x_, zl_, y_, c_):
        return {"row": zh_ * 4 + x_, "blk": zl_ * 8 + y_ * 2 + c_}

    xp = at(zh, (x + 1) % 4, zl, y, c)
    xm = at(zh, (x + 3) % 4, zl, y, c)
    yp = at(zh, x, zl, (y + 1) % 4, c)
    ym = at(zh, x, zl, (y + 3) % 4, c)
    zq = at(zh, x, 1 - zl, y, c)
    zo = at(1 - zh, x, 1 - zl, y, c)
    cp = at(zh, x, zl, y, 1 - c)

    barrier = pltpu.get_barrier_semaphore()
    for d in range(1, 8):
        pl.semaphore_signal(barrier, inc=1, device_id={"row": (row + d) % 8, "blk": blk}, device_id_type=MESH)
    for d in range(1, 16):
        pl.semaphore_signal(barrier, inc=1, device_id={"row": row, "blk": (blk + d) % 16}, device_id_type=MESH)
    pl.semaphore_signal(barrier, inc=1, device_id=zo, device_id_type=MESH)

    def cast(n, _):
        lanes = pl.ds(pl.multiple_of(n * CH, CH), CH)
        part = counts_ref[:, lanes].astype(f32)
        raw[O, :, lanes] = part.astype(bf16)
        own_sum[:, lanes] = jnp.sum(part, axis=0, keepdims=True)
        return 0

    lax.fori_loop(0, NCH, cast, 0)
    pl.semaphore_wait(barrier, 23)

    step1 = [pltpu.make_async_remote_copy(
        src_ref=own_sum, dst_ref=got1.at[d - 1], send_sem=snd1.at[d - 1], recv_sem=rcv1.at[d - 1],
        device_id={"row": (row + d) % 8, "blk": blk}, device_id_type=MESH) for d in range(1, 8)]
    step2 = [pltpu.make_async_remote_copy(
        src_ref=part_sum, dst_ref=got2.at[d - 1], send_sem=snd2.at[d - 1], recv_sem=rcv2.at[d - 1],
        device_id={"row": row, "blk": (blk + d) % 16}, device_id_type=MESH) for d in range(1, 16)]

    copies = {}

    def copy(name, src, dst, device):
        k = len(copies)
        copies[name] = pltpu.make_async_remote_copy(
            src_ref=src, dst_ref=dst, send_sem=ssem.at[k], recv_sem=rsem.at[k],
            device_id=device, device_id_type=MESH)

    def start(*names):
        for name in names:
            copies[name].start()

    def arrived(*names):
        for name in names:
            copies[name].wait_recv()

    def raw_half(slot, h):
        return raw.at[slot, h * HALF:(h + 1) * HALF, :]

    def wz_half(slot, h):
        return wz.at[slot, h * (BINS // 2):(h + 1) * (BINS // 2), :]

    def bb_half(slot, h):
        return bbuf.at[slot * 256 + h * HALF:slot * 256 + (h + 1) * HALF, :]

    def bb_core(slot, h):
        return bbuf.at[slot * 256 + ROWS + h * HALF:slot * 256 + ROWS + (h + 1) * HALF, :]

    def bb_full(slot, other):
        return bbuf.at[slot * 256 + other * ROWS:slot * 256 + (other + 1) * ROWS, :]

    for h in range(2):
        copy(("xp", h), raw_half(O, h), raw_half(XM, h), xp)
        copy(("xm", h), raw_half(O, h), raw_half(XP, h), xm)
        copy(("yp", h), raw_half(O, h), raw_half(YM, h), yp)
        copy(("ym", h), raw_half(O, h), raw_half(YP, h), ym)
        copy(("zq", h), raw_half(O, h), raw_half(QZ, h), zq)
        copy(("zo", h), raw_half(QZ, h), raw_half(PZ, h), zo)
        copy(("pxp", h), wz_half(S_Z, h), wz_half(S_ZM, h), xp)
        copy(("pxm", h), wz_half(S_Z, h), wz_half(S_ZP, h), xm)
        copy(("qyp", h), bb_half(S_Z, h), bb_half(S_ZM, h), yp)
        copy(("qym", h), bb_half(S_Z, h), bb_half(S_ZP, h), ym)
        copy(("cz2", h), bb_half(S_Z2, h), bb_core(S_Z2, h), cp)
    copy("x2p", raw_half(XM, 0), raw_half(X2, 0), xp)
    copy("x2m", raw_half(XP, 1), raw_half(X2, 1), xm)
    copy("y2p", raw_half(YM, 0), raw_half(Y2, 0), yp)
    copy("y2m", raw_half(YP, 1), raw_half(Y2, 1), ym)
    copy("px2p", wz_half(S_ZM, 0), wz_half(S_Z2, 0), xp)
    copy("px2m", wz_half(S_ZP, 1), wz_half(S_Z2, 1), xm)
    copy("qy2p", bb_half(S_ZM, 0), bb_half(S_Z2, 0), yp)
    copy("qy2m", bb_half(S_ZP, 1), bb_half(S_Z2, 1), ym)
    for slot in (S_O, S_Z, S_M, S_P, S_2, S_ZM, S_ZP):
        copy(("c", slot), bb_full(slot, 0), bb_full(slot, 1), cp)

    for s in step1:
        s.start()
    start(("xp", 0), ("xm", 1), ("yp", 0), ("ym", 1), ("zq", 0))

    total = lax.fori_loop(0, TAPS, lambda k, s: s + taps_ref[k], jnp.int32(0)).astype(f32)
    unit = 1.0 / jnp.full((1, 128), total, f32)
    late = lax.broadcasted_iota(jnp.int32, (WIN, CH), 1) + PAD - lax.broadcasted_iota(jnp.int32, (WIN, CH), 0)
    band = jnp.zeros((WIN, CH), f32)
    for k in range(TAPS):
        band = jnp.where(late == k, taps_ref[k].astype(f32), band)
    wrow[...] = band.astype(bf16)
    late = lax.broadcasted_iota(jnp.int32, (CH, WIN), 0) + PAD - lax.broadcasted_iota(jnp.int32, (CH, WIN), 1)
    band = jnp.zeros((CH, WIN), f32)
    for k in range(TAPS):
        band = jnp.where(late == k, taps_ref[k].astype(f32), band)
    wcol[...] = band.astype(bf16)
    ft[BINS:BINS + LAGMAX, :] = jnp.zeros((LAGMAX, 128), f32)
    for k in range(8):
        wz[k, BINS:BINS + LAGMAX, :] = jnp.zeros((LAGMAX, 128), bf16)

    for s in step1:
        s.wait_recv()
    part_sum[...] = own_sum[...] + sum(got1[d] for d in range(7))
    for s in step2:
        s.start()
    start(("xp", 1), ("xm", 0), ("yp", 1), ("ym", 0), ("zq", 1))

    arrived(("xp", 0), ("xm", 1))
    start("x2p", "x2m")
    arrived(("yp", 0), ("ym", 1))
    start("y2p", "y2m")
    arrived(("zq", 0))
    start(("zo", 0))

    for s in step2:
        s.wait_recv()
    alls = part_sum[...] + sum(got2[d] for d in range(15))
    high = alls.astype(bf16)
    rest = alls - high.astype(f32)
    mid = rest.astype(bf16)
    low = (rest - mid.astype(f32)).astype(bf16)
    psum_r = jnp.zeros((8, CH), f32)
    psum_t = jnp.zeros((8, 128), f32)
    edge = jnp.zeros((1, PAD), bf16)
    for n in range(NCH):
        smooth_r = jnp.zeros((16, CH), f32)
        smooth_t = jnp.zeros((CH, 128), f32)
        for piece in (high, mid, low):
            if n == 0:
                win = jnp.concatenate([edge, piece[:, 0:CH]], axis=1)
            else:
                win = piece[:, n * CH - PAD:(n + 1) * CH]
            smooth_r += jnp.dot(jnp.broadcast_to(win, (16, WIN)), wrow[...], preferred_element_type=f32)
            smooth_t += lax.dot_general(wcol[...], jnp.broadcast_to(win, (128, WIN)), (((1,), (1,)), ((), ())),
                                        preferred_element_type=f32)
        popr[:, n * CH:(n + 1) * CH] = smooth_r[0:8]
        popt[n * CH:(n + 1) * CH, :] = smooth_t
        psum_r += smooth_r[0:8]
        psum_t += jnp.sum(smooth_t.reshape(CH // 8, 8, 128), axis=0)
    mean_r = jnp.sum(psum_r, axis=1, keepdims=True) * (1.0 / BINS)
    mean_t = jnp.sum(psum_t, axis=0, keepdims=True) * (1.0 / BINS)
    share = unit * (1.0 / NEURONS)
    popr[...] = (popr[...] - mean_r) * share[:, 0:1]

    def pop_column(n, _):
        rows = pl.ds(pl.multiple_of(n * CH, CH), CH)
        popt[rows, :] = (popt[rows, :] - mean_t) * share
        return 0

    lax.fori_loop(0, NCH, pop_column, 0)

    def to_rows(src, slot):
        dst = slice(slot * 256, slot * 256 + ROWS)

        got = jnp.dot(raw[src, :, 0:CH], wrow[PAD:WIN, :], preferred_element_type=f32)
        fr[:, 0:CH] = got

        def smooth(n, s):
            win = raw[src, :, pl.ds(pl.multiple_of(n * CH - PAD, PAD), WIN)]
            got = jnp.dot(win, wrow[...], preferred_element_type=f32)
            fr[:, pl.ds(pl.multiple_of(n * CH, CH), CH)] = got
            return s + got[:, 0:128] + got[:, 128:256]

        s = lax.fori_loop(1, NCH, smooth, got[:, 0:128] + got[:, 128:256])
        mean = jnp.sum(s, axis=1, keepdims=True) * (1.0 / BINS)

        def centre(n, q):
            lanes = pl.ds(pl.multiple_of(n * CH, CH), CH)
            r = (fr[:, lanes] - mean) * unit[:, 0:1] - popr[0:1, lanes]
            fr[:, lanes] = r
            r = r * r
            return q + r[:, 0:128] + r[:, 128:256]

        q = lax.fori_loop(0, NCH, centre, jnp.zeros((ROWS, 128), f32))
        scale = lax.rsqrt(jnp.sum(q, axis=1, keepdims=True) * (1.0 / BINS) + 1e-05)

        def put(n, _):
            lanes = pl.ds(pl.multiple_of(n * CH, CH), CH)
            bbuf[dst, lanes] = (fr[:, lanes] * scale).astype(bf16)
            return 0

        lax.fori_loop(0, NCH, put, 0)

    lag = lag_ref[0]

    def to_columns(src, slot):
        got = lax.dot_general(wcol[:, PAD:WIN], raw[src, :, 0:CH], (((1,), (1,)), ((), ())),
                              preferred_element_type=f32)
        ft[0:CH, :] = got

        def smooth(n, s):
            win = raw[src, :, pl.ds(pl.multiple_of(n * CH - PAD, PAD), WIN)]
            got = lax.dot_general(wcol[...], win, (((1,), (1,)), ((), ())), preferred_element_type=f32)
            ft[pl.ds(pl.multiple_of(n * CH, CH), CH), :] = got
            return s + jnp.sum(got.reshape(CH // 8, 8, 128), axis=0)

        s = lax.fori_loop(1, NCH, smooth, jnp.sum(got.reshape(CH // 8, 8, 128), axis=0))
        mean = jnp.sum(s, axis=0, keepdims=True) * (1.0 / BINS)

        def centre(n, q):
            rows = pl.ds(pl.multiple_of(n * CH, CH), CH)
            r = (ft[rows, :] - mean) * unit - popt[rows, :]
            ft[rows, :] = r
            return q + jnp.sum((r * r).reshape(CH // 8, 8, 128), axis=0)

        q = lax.fori_loop(0, NCH, centre, jnp.zeros((8, 128), f32))
        scale = lax.rsqrt(jnp.sum(q, axis=0, keepdims=True) * (1.0 / BINS) + 1e-05) * (1.0 / BINS)

        def put(n, _):
            first = pl.multiple_of(n * CH, CH)
            wz[slot, pl.ds(first, CH), :] = (ft[pl.ds(first, CH), :] * scale).astype(bf16)
            ws[slot, pl.ds(first, CH), :] = (ft[pl.ds(first + lag, CH), :] * scale).astype(bf16)
            return 0

        lax.fori_loop(0, NCH, put, 0)

    def move(slot):
        def widen(n, _):
            rows = pl.ds(pl.multiple_of(n * CH, CH), CH)
            ft[rows, :] = wz[slot, rows, :].astype(f32)
            return 0

        def put(n, _):
            first = pl.multiple_of(n * CH, CH)
            ws[slot, pl.ds(first, CH), :] = ft[pl.ds(first + lag, CH), :].astype(bf16)
            return 0

        lax.fori_loop(0, NCH, widen, 0)
        lax.fori_loop(0, NCH, put, 0)

    def place(s, major, minor):
        j, i = s // 2, s % 2
        z = (major + i * ((j + 1) % 2) + j // 3) % 2
        return z * 4 + (minor + (j % 2) * (3 + 2 * i) + (j // 2) * (1 - j % 2) * 2) % 4

    def product(s, pairs, g):
        rows = pairs * 256
        left = bbuf[s * 256:s * 256 + rows, :]
        right = jnp.concatenate([ws[g], wz[g, LAGMAX:LAGMAX + BINS, :]], axis=1)
        out = jnp.dot(left, right, preferred_element_type=f32)
        gg = place(g, zh, x)
        for k in range(2 * pairs):
            here = place(s + k // 2, zl, y) * 2 + (c if k % 2 == 0 else 1 - c)
            there = pl.ds(pl.multiple_of(here * ROWS, ROWS), ROWS)
            part = out[k * ROWS:(k + 1) * ROWS]
            acc_ref[0, gg, there, :] = part[:, 0:128].astype(bf16)
            acc_ref[1, gg, there, :] = part[:, 128:256].astype(bf16)

    def products(s, pairs, first, count):
        def one(g, _):
            product(s, pairs, g)
            return 0
        lax.fori_loop(first, first + count, one, 0)

    to_rows(O, S_O)
    start(("c", S_O))
    to_columns(O, S_O)

    arrived(("zq", 1))
    start(("zo", 1))
    to_rows(QZ, S_Z)
    start(("qyp", 0), ("qyp", 1), ("qym", 1), ("qym", 0), ("c", S_Z))
    arrived(("xp", 1), ("xm", 0), ("yp", 1), ("ym", 0))
    arrived(("zo", 0), ("zo", 1))
    to_columns(PZ, S_Z)
    start(("pxp", 0), ("pxp", 1), ("pxm", 1), ("pxm", 0))
    to_rows(YM, S_M)
    start(("c", S_M))
    to_rows(YP, S_P)
    start(("c", S_P))
    to_columns(XM, S_M)
    to_columns(XP, S_P)
    arrived(("c", S_O), ("c", S_Z))
    products(S_O, 2, 0, 4)
    arrived(("c", S_M), ("c", S_P))
    products(S_M, 2, 0, 4)
    arrived("x2p", "x2m", "y2p", "y2m")
    to_rows(Y2, S_2)
    start(("c", S_2))
    to_columns(X2, S_2)
    arrived(("c", S_2))
    products(S_2, 1, 0, 5)
    products(S_O, 2, S_2, 1)
    products(S_M, 2, S_2, 1)
    arrived(("qyp", 0), ("qym", 1), ("pxp", 0), ("pxm", 1))
    start("qy2p", "qy2m", "px2p", "px2m")
    arrived(("qyp", 1), ("qym", 0), ("pxp", 1), ("pxm", 0))
    start(("c", S_ZM), ("c", S_ZP))
    move(S_ZM)
    move(S_ZP)
    products(S_O, 2, S_ZM, 2)
    products(S_M, 2, S_ZM, 2)
    products(S_2, 1, S_ZM, 2)
    arrived(("c", S_ZM), ("c", S_ZP))
    products(S_ZM, 2, 0, 5)
    products(S_ZM, 2, S_ZM, 2)
    arrived("qy2p", "qy2m")
    start(("cz2", 0), ("cz2", 1))
    arrived("px2p", "px2m")
    move(S_Z2)
    products(S_O, 2, S_Z2, 1)
    products(S_M, 2, S_Z2, 1)
    products(S_ZM, 2, S_Z2, 1)
    products(S_2, 1, S_Z2, 1)
    arrived(("cz2", 0), ("cz2", 1))
    products(S_Z2, 1, 0, 8)

    for s in step1 + step2:
        s.wait_send()
    for name in copies:
        copies[name].wait_send()


N_COPIES = 2 * 11 + 8 + 7


def gathered(taps, lags, counts):
    smem = pl.BlockSpec(memory_space=pltpu.SMEM)
    vmem = pl.BlockSpec(memory_space=pltpu.VMEM)
    dma = pltpu.SemaphoreType.DMA
    return pl.pallas_call(
        gather_kernel,
        out_shape=jax.ShapeDtypeStruct((2, 8, 2048, 128), bf16),
        in_specs=[smem, smem, vmem],
        out_specs=vmem,
        scratch_shapes=[
            pltpu.VMEM((9, ROWS, BINS), bf16),
            pltpu.VMEM((2048, BINS), bf16),
            pltpu.VMEM((8, BINS + LAGMAX, 128), bf16),
            pltpu.VMEM((8, BINS, 128), bf16),
            pltpu.VMEM((BINS + LAGMAX, 128), f32),
            pltpu.VMEM((ROWS, BINS), f32),
            pltpu.VMEM((BINS, 128), f32),
            pltpu.VMEM((8, BINS), f32),
            pltpu.VMEM((WIN, CH), bf16),
            pltpu.VMEM((CH, WIN), bf16),
            pltpu.VMEM((1, BINS), f32),
            pltpu.VMEM((1, BINS), f32),
            pltpu.VMEM((7, 1, BINS), f32),
            pltpu.VMEM((15, 1, BINS), f32),
            dma((7,)), dma((7,)), dma((15,)), dma((15,)),
            dma((N_COPIES,)), dma((N_COPIES,)),
        ],
        compiler_params=pltpu.CompilerParams(
            collective_id=0, has_side_effects=True, vmem_limit_bytes=44 << 20),
        name="gather_products",
    )(taps, lags, counts)


def layout_kernel(acc_ref, out_ref):
    out_ref[0] = jnp.swapaxes(acc_ref[0].astype(f32), 0, 1).astype(bf16)


def laid_out(acc):
    rows = 512
    return pl.pallas_call(
        layout_kernel,
        out_shape=jax.ShapeDtypeStruct((2, 2048, 8, 128), bf16),
        grid=(2, 2048 // rows),
        in_specs=[pl.BlockSpec((1, 8, rows, 128), lambda l, i: (l, 0, i, 0))],
        out_specs=pl.BlockSpec((1, rows, 8, 128), lambda l, i: (l, i, 0, 0)),
        compiler_params=pltpu.CompilerParams(vmem_limit_bytes=16 << 20),
        name="layout",
    )(acc)


def shards(spike_counts, kernel_taps, lag_bins):
    return laid_out(gathered(kernel_taps, lag_bins, spike_counts))


def solution(mesh):
    placed = (P(("row", "blk"), None), P(), P())
    return jax.shard_map(
        shards, mesh=mesh, in_specs=placed, out_specs=P(None, "row", None, "blk"), check_vma=False
    )
```

time: 260 us -> 83.1 us (0.32)
  waiting for transfers between devices: 106 us -> 0 us
  Pallas kernels: 0 us -> 80.4 us
  blocking collectives: 68.7 us -> 0 us
  matrix products: 23.8 us -> 0 us
  local copies, waits for them, and re-layouts: 23.9 us -> 2.53 us
  other arithmetic: 19.5 us -> 0 us
  between operations: 17.2 us -> 0.01 us
    all_gather x2 -> x0, waiting for transfers between devices: 105 us -> none  [the longest x1 62.5 us: shards(): columns = lax.all_gather(zscored, 'row', axis=0, tiled=True)]
    pallas_call x0 -> x2, Pallas kernels: none -> 80.4 us  [the longest x1 73.9 us: gathered(): pl.pallas_call(gather_kernel, out_shape=jax.ShapeDtypeStruct((2, 8, 2048,...]
    psum x1 -> x0, blocking collectives: 68.7 us -> none  [shards(): totals = lax.psum(jnp.sum(centred, axis=0), ('row', 'blk'))]
    dot_general x1 -> x0, matrix products: 23.8 us -> none  [shards(): jnp.dot(piece, stacked.T, preferred_element_type=jnp.float32) / BINS]
    reduce_sum x4 -> x0, other arithmetic: 15.8 us -> none  [the longest x1 14.1 us: shards(): centred = smooth - jnp.mean(smooth, axis=1, keepdims=True)]
    convert_element_type x1 -> x0, local copies, waits for them, and re-layouts: 12.6 us -> none  [shards(): return jnp.transpose(product, (1, 0, 2, 3)).astype(jnp.bfloat16)]
    dynamic_slice x1 -> x0, local copies, waits for them, and re-layouts: 9.97 us -> none  [later_bins(): return lax.dynamic_slice_in_dim(padded, lag, BINS, 1)]
  transfers between devices with their start and end apart: 2 -> 0, of which waited for: 2 -> 0; matrix products, arithmetic and copies ran while one was open for 4% -> 0% of each run, Pallas kernels for 0% -> 0%
where the time goes in v1:
time: 83.1 us; the launch traced here: 82.9 us
  Pallas kernels  80.4 us (97%)
  local copies, waits for them, and re-layouts  2.53 us (3%)
    pallas_call x1, Pallas kernels, gathered(): pl.pallas_call(gather_kernel, out_shape=jax.ShapeDtypeStruct((2, 8, 2048,...  73.9 us
    pallas_call x1, Pallas kernels, laid_out(): pl.pallas_call(layout_kernel, out_shape=jax.ShapeDtypeStruct((2, 2048, 8,...  6.49 us
    unnamed x6, local copies, waits for them, and re-layouts  2.53 us

profile of v1, /device:TPU:1, one launch (start us, length us, event | category | flops | bytes accessed | tf_op | source)
XLA Modules:
  0.0 82.9 jit_solution(6860012829485182987)
XLA Ops:
  0.0 0.0 copy-start
  0.0 1.2 %copy-done = s32[128,2048]{1,0:T(8,128)S(1)} copy-done((s32[128,2048]{1,0:T(8,128)S(1)}, s32[128,2048]{1,0:T(8,128)}, u32[]{:S(2)}) %copy-start) | copy-done | bytes 1048600
  1.2 0.0 copy-start.1
  1.2 0.7 copy-done.1
  1.9 0.0 copy-start.2
  1.9 0.7 copy-done.2
  2.5 73.9 %gather_products.1.acc_ref = bf16[2,8,2048,128]{3,2,1,0:T(8,128)(2,1)S(1)} custom-call(s32[16]{0:T(128)S(1)} %copy-done.1, s32[2]{0:T(128)S(1)} %copy-done.2, s32[128,2048]{1,0:T(8,128)S(1)} %copy-done), custom_call_target="tpu_custom_call" | custom-call | tf_op jit(solution)/shard_map/gather_products/pallas_call | solution.py:366
  76.4 6.5 %layout.1 = bf16[2,2048,8,128]{3,2,1,0:T(8,128)(2,1)} custom-call(bf16[2,8,2048,128]{3,2,1,0:T(8,128)(2,1)S(1)} %gather_products.1.acc_ref), custom_call_target="tpu_custom_call" | custom-call | tf_op jit(solution)/shard_map/layout/pallas_call | solution.py:401
Async XLA Ops:
  0.0 1.2 %copy-start = (s32[128,2048]{1,0:T(8,128)S(1)}, s32[128,2048]{1,0:T(8,128)}, u32[]{:S(2)}) copy-start(s32[128,2048]{1,0:T(8,128)} %counts_ref.1) | copy-start | bytes 3145732
  1.2 0.7 copy-start.1
  1.9 0.7 copy-start.2

commit v2 on v1

v2 whole, which is shorter than its diff:
```python
import functools

import jax
import jax.numpy as jnp
from jax import lax
from jax.experimental import pallas as pl
from jax.experimental.pallas import tpu as pltpu
from jax.sharding import PartitionSpec as P

NEURONS = 16384
BINS = 2048
TAPS = 16
LAGMAX = 32
MESH = pl.DeviceIdType.MESH
f32 = jnp.float32
bf16 = jnp.bfloat16

ROWS = 128
HALF = ROWS // 2
PAD = 128
CH = 256
NCH = BINS // CH
WIN = CH + PAD
QUARTER = ROWS // 4

O, XM, XP, X2, PZ, YM, YP, Y2, QZ = range(9)
S_O, S_Z, S_M, S_P, S_2, S_Z2, S_ZM, S_ZP = range(8)


def gather_kernel(taps_hbm, lag_hbm, counts_hbm, acc_ref,
                  taps_ref, lag_ref, counts, raw, bbuf, wz, ws, ft, fr, popt, popr, wrow, wcol, wsum,
                  own_sum, part_sum, got1, got2, lsem, snd1, rcv1, snd2, rcv2, ssem, rsem):
    row = lax.axis_index("row")
    blk = lax.axis_index("blk")
    zh, x = row // 4, row % 4
    zl, y, c = blk // 8, (blk // 2) % 4, blk % 2

    loads = [pltpu.make_async_copy(counts_hbm.at[h * HALF:(h + 1) * HALF, :],
                                   counts.at[h * HALF:(h + 1) * HALF, :], lsem.at[h]) for h in range(2)]
    loads += [pltpu.make_async_copy(taps_hbm, taps_ref, lsem.at[2]),
              pltpu.make_async_copy(lag_hbm, lag_ref, lsem.at[3])]
    for load in loads:
        load.start()

    def at(zh_, x_, zl_, y_, c_):
        return {"row": zh_ * 4 + x_, "blk": zl_ * 8 + y_ * 2 + c_}

    xp = at(zh, (x + 1) % 4, zl, y, c)
    xm = at(zh, (x + 3) % 4, zl, y, c)
    yp = at(zh, x, zl, (y + 1) % 4, c)
    ym = at(zh, x, zl, (y + 3) % 4, c)
    zq = at(zh, x, 1 - zl, y, c)
    zo = at(1 - zh, x, 1 - zl, y, c)
    cp = at(zh, x, zl, y, 1 - c)

    barrier = pltpu.get_barrier_semaphore()
    for d in range(1, 8):
        pl.semaphore_signal(barrier, inc=1, device_id={"row": (row + d) % 8, "blk": blk}, device_id_type=MESH)
    for d in range(1, 16):
        pl.semaphore_signal(barrier, inc=1, device_id={"row": row, "blk": (blk + d) % 16}, device_id_type=MESH)
    pl.semaphore_signal(barrier, inc=1, device_id=zo, device_id_type=MESH)

    for h in range(2):
        loads[h].wait()
        for n in range(NCH):
            part = counts[h * HALF:(h + 1) * HALF, n * CH:(n + 1) * CH].astype(f32)
            raw[O, h * HALF:(h + 1) * HALF, n * CH:(n + 1) * CH] = part.astype(bf16)
            part = jnp.sum(part, axis=0, keepdims=True)
            own_sum[:, n * CH:(n + 1) * CH] = part if h == 0 else own_sum[:, n * CH:(n + 1) * CH] + part
    pl.semaphore_wait(barrier, 23)

    step1 = [pltpu.make_async_remote_copy(
        src_ref=own_sum, dst_ref=got1.at[d - 1], send_sem=snd1.at[d - 1], recv_sem=rcv1.at[d - 1],
        device_id={"row": (row + d) % 8, "blk": blk}, device_id_type=MESH) for d in range(1, 8)]
    step2 = [pltpu.make_async_remote_copy(
        src_ref=part_sum, dst_ref=got2.at[d - 1], send_sem=snd2.at[d - 1], recv_sem=rcv2.at[d - 1],
        device_id={"row": row, "blk": (blk + d) % 16}, device_id_type=MESH) for d in range(1, 16)]

    copies = {}

    def copy(name, src, dst, device):
        k = len(copies)
        copies[name] = pltpu.make_async_remote_copy(
            src_ref=src, dst_ref=dst, send_sem=ssem.at[k], recv_sem=rsem.at[k],
            device_id=device, device_id_type=MESH)

    def start(*names):
        for name in names:
            copies[name].start()

    def arrived(*names):
        for name in names:
            copies[name].wait_recv()

    def raw_half(slot, h):
        return raw.at[slot, h * HALF:(h + 1) * HALF, :]

    def raw_quarter(slot, k):
        return raw.at[slot, k * QUARTER:(k + 1) * QUARTER, :]

    def wz_half(slot, h):
        return wz.at[slot, h * (BINS // 2):(h + 1) * (BINS // 2), :]

    def bb_half(slot, h, other=0):
        first = slot * 256 + other * ROWS + h * HALF
        return bbuf.at[first:first + HALF, :]

    for h in range(2):
        copy(("xp", h), raw_half(O, h), raw_half(XM, h), xp)
        copy(("xm", h), raw_half(O, h), raw_half(XP, h), xm)
        copy(("yp", h), raw_half(O, h), raw_half(YM, h), yp)
        copy(("ym", h), raw_half(O, h), raw_half(YP, h), ym)
        copy(("pxp", h), wz_half(S_Z, h), wz_half(S_ZM, h), xp)
        copy(("pxm", h), wz_half(S_Z, h), wz_half(S_ZP, h), xm)
        copy(("qyp", h), bb_half(S_Z, h), bb_half(S_ZM, h), yp)
        copy(("qym", h), bb_half(S_Z, h), bb_half(S_ZP, h), ym)
        copy(("zy", h), bb_half(S_2, h), bb_half(S_Z2, h), zq)
        for slot in (S_Z2, S_ZM, S_ZP):
            copy(("c", slot, h), bb_half(slot, h), bb_half(slot, h, 1), cp)
    for k in range(4):
        copy(("zq", k), raw_quarter(O, k), raw_quarter(QZ, k), zq)
        copy(("zo", k), raw_quarter(QZ, k), raw_quarter(PZ, k), zo)
    copy("x2p", raw_half(XM, 0), raw_half(X2, 0), xp)
    copy("x2m", raw_half(XP, 1), raw_half(X2, 1), xm)
    copy("y2p", raw_half(YM, 0), raw_half(Y2, 0), yp)
    copy("y2m", raw_half(YP, 1), raw_half(Y2, 1), ym)
    copy("px2p", wz_half(S_ZM, 0), wz_half(S_Z2, 0), xp)
    copy("px2m", wz_half(S_ZP, 1), wz_half(S_Z2, 1), xm)
    for slot in (S_O, S_Z, S_M, S_P, S_2):
        copy(("c", slot), bbuf.at[slot * 256:slot * 256 + ROWS, :],
             bbuf.at[slot * 256 + ROWS:slot * 256 + 2 * ROWS, :], cp)

    for s in step1:
        s.start()
    start(("zq", 0), ("xp", 0), ("xm", 1), ("yp", 0), ("ym", 1), ("zq", 1))

    loads[2].wait()
    loads[3].wait()
    taps = [taps_ref[k].astype(f32) for k in range(TAPS)]
    total = sum(taps[1:], taps[0])
    unit = 1.0 / jnp.full((8, 128), total, f32)
    late = lax.broadcasted_iota(jnp.int32, (WIN, CH), 1) + PAD - lax.broadcasted_iota(jnp.int32, (WIN, CH), 0)
    band = jnp.zeros((WIN, CH), f32)
    for k in range(TAPS):
        band = jnp.where(late == k, taps[k], band)
    wrow[...] = band.astype(bf16)
    late = lax.broadcasted_iota(jnp.int32, (CH, WIN), 0) + PAD - lax.broadcasted_iota(jnp.int32, (CH, WIN), 1)
    band = jnp.zeros((CH, WIN), f32)
    for k in range(TAPS):
        band = jnp.where(late == k, taps[k], band)
    wcol[...] = band.astype(bf16)
    wsum[...] = jnp.full((BINS, 128), total, f32).astype(bf16)
    left = TAPS - lax.broadcasted_iota(jnp.int32, (TAPS, 128), 0)
    edge = jnp.zeros((TAPS, 128), f32)
    for k in range(TAPS):
        edge = edge + jnp.where(left > k, taps[k], 0.0)
    wsum[BINS - TAPS:BINS, :] = edge.astype(bf16)
    ft[BINS:BINS + LAGMAX, :] = jnp.zeros((LAGMAX, 128), f32)
    for k in range(8):
        wz[k, BINS:BINS + LAGMAX, :] = jnp.zeros((LAGMAX, 128), bf16)

    for s in step1:
        s.wait_recv()
    part_sum[...] = own_sum[...] + sum([got1[d] for d in range(1, 7)], got1[0])
    for s in step2:
        s.start()
    start(("zq", 2), ("xp", 1), ("xm", 0), ("yp", 1), ("ym", 0), ("zq", 3))
    arrived(("zq", 0))
    start(("zo", 0))
    arrived(("xp", 0), ("xm", 1))
    start("x2p", "x2m")
    arrived(("yp", 0), ("ym", 1))
    start("y2p", "y2m")
    arrived(("zq", 1))
    start(("zo", 1))

    for s in step2:
        s.wait_recv()
    alls = part_sum[...] + sum([got2[d] for d in range(1, 15)], got2[0])
    high = alls.astype(bf16)
    rest = alls - high.astype(f32)
    mid = rest.astype(bf16)
    low = (rest - mid.astype(f32)).astype(bf16)
    summed = jnp.zeros((8, 128), f32)
    for n in range(NCH):
        first = max(n * CH - PAD, 0)
        wins = jnp.concatenate(
            [jnp.broadcast_to(piece[:, first:(n + 1) * CH], (16, (n + 1) * CH - first)) for piece in (high, mid, low)],
            axis=0)
        got = jnp.dot(wins, wrow[PAD:WIN, :] if n == 0 else wrow[...], preferred_element_type=f32)
        got = (got[0:8] + got[16:24]) + got[32:40]
        popr[:, n * CH:(n + 1) * CH] = got
        summed = summed + (got[:, 0:128] + got[:, 128:256])
    mean_pop = jnp.sum(summed, axis=1, keepdims=True) * (1.0 / BINS)
    popr[...] = (popr[...] - mean_pop) * (1.0 / NEURONS)
    for n in range(BINS // 128):
        popt[n * 128:(n + 1) * 128, :] = jnp.transpose(
            jnp.broadcast_to(popr[0:1, n * 128:(n + 1) * 128], (128, 128)))

    def to_rows(src, slot):
        mean = jnp.dot(raw[src], wsum[...], preferred_element_type=f32) * (1.0 / BINS)
        mean = jnp.concatenate([mean, mean], axis=1)
        q = jnp.zeros((ROWS, 128), f32)
        for n in range(NCH):
            if n == 0:
                got = jnp.dot(raw[src, :, 0:CH], wrow[PAD:WIN, :], preferred_element_type=f32)
            else:
                got = jnp.dot(raw[src, :, n * CH - PAD:(n + 1) * CH], wrow[...], preferred_element_type=f32)
            r = got - mean - popr[0:1, n * CH:(n + 1) * CH]
            fr[:, n * CH:(n + 1) * CH] = r
            r = r * r
            q = q + r[:, 0:128] + r[:, 128:256]
        u = unit[0:1, 0:1]
        scale = lax.rsqrt(jnp.sum(q, axis=1, keepdims=True) * (1.0 / BINS) * (u * u) + 1e-05) * u
        for n in range(NCH):
            bbuf[slot * 256:slot * 256 + ROWS, n * CH:(n + 1) * CH] = (
                fr[:, n * CH:(n + 1) * CH] * scale).astype(bf16)

    lag = lag_ref[0]

    def to_columns(src, slot):
        mean = jnp.transpose(jnp.dot(raw[src], wsum[...], preferred_element_type=f32) * (1.0 / BINS))[0:8]
        q = jnp.zeros((4, 8, 128), f32)
        for n in range(NCH):
            if n == 0:
                got = lax.dot_general(wcol[:, PAD:WIN], raw[src, :, 0:CH], (((1,), (1,)), ((), ())),
                                      preferred_element_type=f32)
            else:
                got = lax.dot_general(wcol[...], raw[src, :, n * CH - PAD:(n + 1) * CH], (((1,), (1,)), ((), ())),
                                      preferred_element_type=f32)
            r = got.reshape(32, 8, 128) - mean[None] - popt[n * CH:(n + 1) * CH, :].reshape(32, 8, 128)
            ft[n * CH:(n + 1) * CH, :] = r.reshape(CH, 128)
            r = r * r
            for j in range(8):
                q = q + r[4 * j:4 * j + 4]
        q = (q[0] + q[1]) + (q[2] + q[3])
        u = unit[0:1]
        scale = lax.rsqrt(jnp.sum(q, axis=0, keepdims=True) * (1.0 / BINS) * (u * u) + 1e-05) * u * (1.0 / BINS)
        for n in range(NCH):
            wz[slot, n * CH:(n + 1) * CH, :] = (ft[n * CH:(n + 1) * CH, :] * scale).astype(bf16)
            ws[slot, n * CH:(n + 1) * CH, :] = (ft[pl.ds(n * CH + lag, CH), :] * scale).astype(bf16)

    def move(slot):
        for n in range(NCH):
            ft[n * CH:(n + 1) * CH, :] = wz[slot, n * CH:(n + 1) * CH, :].astype(f32)
        for n in range(NCH):
            ws[slot, n * CH:(n + 1) * CH, :] = ft[pl.ds(n * CH + lag, CH), :].astype(bf16)

    def place(s, major, minor):
        j, i = s // 2, s % 2
        z = (major + i * ((j + 1) % 2) + j // 3) % 2
        return z * 4 + (minor + (j % 2) * (3 + 2 * i) + (j // 2) * (1 - j % 2) * 2) % 4

    def whole(s, pairs=1):
        return [(s * 256 + k * ROWS, ROWS, (place(s + k // 2, zl, y) * 2 + (c if k % 2 == 0 else 1 - c)) * ROWS)
                for k in range(2 * pairs)]

    def halves(s, h):
        return [(s * 256 + k * ROWS + h * HALF, HALF, (place(s, zl, y) * 2 + (c if k == 0 else 1 - c)) * ROWS + h * HALF)
                for k in range(2)]

    def multiply(segments, groups):
        runs = []
        for first, size, _ in segments:
            if runs and isinstance(first, int) and runs[-1][0] + runs[-1][1] == first:
                runs[-1][1] += size
            else:
                runs.append([first, size])
        left = [bbuf[first:first + size, :] if isinstance(first, int) else bbuf[pl.ds(first, size), :]
                for first, size in runs]
        left = left[0] if len(left) == 1 else jnp.concatenate(left, axis=0)
        for g in groups:
            right = jnp.concatenate([ws[g], wz[g, LAGMAX:LAGMAX + BINS, :]], axis=1)
            out = jnp.dot(left, right, preferred_element_type=f32)
            gg, k = place(g, zh, x), 0
            for _, size, there in segments:
                there = pl.ds(pl.multiple_of(there, size), size)
                acc_ref[0, gg, there, :] = out[k:k + size, 0:128].astype(bf16)
                acc_ref[1, gg, there, :] = out[k:k + size, 128:256].astype(bf16)
                k += size

    def multiply_pairs(first, count, pairs, groups):
        def one(n, _):
            s = first + n * pairs
            start_row = pl.multiple_of(s * 256, 256)
            left = bbuf[pl.ds(start_row, pairs * 256), :]
            for g in groups:
                right = jnp.concatenate([ws[g], wz[g, LAGMAX:LAGMAX + BINS, :]], axis=1)
                out = jnp.dot(left, right, preferred_element_type=f32)
                gg = place(g, zh, x)
                for k, (_, size, there) in enumerate(whole(s, pairs)):
                    there = pl.ds(pl.multiple_of(there, size), size)
                    acc_ref[0, gg, there, :] = out[k * size:(k + 1) * size, 0:128].astype(bf16)
                    acc_ref[1, gg, there, :] = out[k * size:(k + 1) * size, 128:256].astype(bf16)
            return 0
        lax.fori_loop(0, count, one, 0)

    to_rows(O, S_O)
    start(("c", S_O))
    arrived(("zq", 2))
    start(("zo", 2))
    to_columns(O, S_O)
    arrived(("zq", 3))
    start(("zo", 3))
    to_rows(QZ, S_Z)
    start(("qyp", 0), ("qym", 1), ("qyp", 1), ("qym", 0), ("c", S_Z))
    arrived(("xp", 1), ("xm", 0), ("yp", 1), ("ym", 0))
    to_rows(YM, S_M)
    start(("c", S_M))
    to_rows(YP, S_P)
    start(("c", S_P))
    to_columns(XM, S_M)
    to_columns(XP, S_P)
    arrived(("zo", 0), ("zo", 1), ("zo", 2), ("zo", 3))
    to_columns(PZ, S_Z)
    start(("pxp", 0), ("pxm", 1), ("pxp", 1), ("pxm", 0))
    arrived(("c", S_O), ("c", S_Z))
    multiply_pairs(S_O, 2, 1, (S_O, S_Z, S_M, S_P))
    arrived("y2p", "y2m")
    to_rows(Y2, S_2)
    start(("zy", 0), ("zy", 1), ("c", S_2))
    arrived("x2p", "x2m")
    to_columns(X2, S_2)
    arrived(("c", S_M), ("c", S_P), ("c", S_2))
    multiply_pairs(S_M, 3, 1, (S_O, S_Z, S_M, S_P))
    multiply(whole(S_O, 5), (S_2,))
    arrived(("qyp", 0), ("qym", 1))
    start(("c", S_ZM, 0), ("c", S_ZP, 1))
    arrived(("pxp", 0), ("pxm", 1))
    start("px2p", "px2m")
    arrived(("c", S_ZM, 0), ("c", S_ZP, 1))
    multiply(halves(S_ZM, 0) + halves(S_ZP, 1), (S_O, S_Z, S_M, S_P, S_2))
    arrived(("qyp", 1), ("qym", 0))
    start(("c", S_ZM, 1), ("c", S_ZP, 0))
    arrived(("pxp", 1), ("pxm", 0))
    move(S_ZM)
    move(S_ZP)
    multiply_pairs(S_O, 2, 2, (S_ZM, S_ZP))
    arrived(("zy", 0), ("zy", 1))
    start(("c", S_Z2, 0), ("c", S_Z2, 1))
    arrived(("c", S_ZM, 1), ("c", S_ZP, 0))
    multiply(halves(S_ZM, 1) + halves(S_ZP, 0), (S_O, S_Z, S_M, S_P, S_2))
    multiply(whole(S_2) + whole(S_ZM, 2), (S_ZM, S_ZP))
    arrived(("c", S_Z2, 0), ("c", S_Z2, 1))
    multiply(whole(S_Z2), (S_O, S_Z, S_M, S_P, S_2, S_ZM, S_ZP))
    arrived("px2p", "px2m")
    move(S_Z2)
    multiply_pairs(S_O, 2, 4, (S_Z2,))

    for s in step1 + step2:
        s.wait_send()
    for name in copies:
        copies[name].wait_send()


N_COPIES = 2 * 12 + 8 + 6 + 5


def gathered(taps, lags, counts):
    dma = pltpu.SemaphoreType.DMA
    return pl.pallas_call(
        gather_kernel,
        out_shape=jax.ShapeDtypeStruct((2, 8, 2048, 128), bf16),
        in_specs=[pl.BlockSpec(memory_space=pltpu.HBM)] * 3,
        out_specs=pl.BlockSpec(memory_space=pltpu.VMEM),
        scratch_shapes=[
            pltpu.SMEM((TAPS,), jnp.int32),
            pltpu.SMEM((2,), jnp.int32),
            pltpu.VMEM((ROWS, BINS), jnp.int32),
            pltpu.VMEM((9, ROWS, BINS), bf16),
            pltpu.VMEM((2048, BINS), bf16),
            pltpu.VMEM((8, BINS + LAGMAX, 128), bf16),
            pltpu.VMEM((8, BINS, 128), bf16),
            pltpu.VMEM((BINS + LAGMAX, 128), f32),
            pltpu.VMEM((ROWS, BINS), f32),
            pltpu.VMEM((BINS, 128), f32),
            pltpu.VMEM((8, BINS), f32),
            pltpu.VMEM((WIN, CH), bf16),
            pltpu.VMEM((CH, WIN), bf16),
            pltpu.VMEM((BINS, 128), bf16),
            pltpu.VMEM((1, BINS), f32),
            pltpu.VMEM((1, BINS), f32),
            pltpu.VMEM((7, 1, BINS), f32),
            pltpu.VMEM((15, 1, BINS), f32),
            dma((4,)), dma((7,)), dma((7,)), dma((15,)), dma((15,)),
            dma((N_COPIES,)), dma((N_COPIES,)),
        ],
        compiler_params=pltpu.CompilerParams(
            collective_id=0, has_side_effects=True, vmem_limit_bytes=44 << 20),
        name="gather_products",
    )(*(pltpu.with_memory_space_constraint(a, pltpu.HBM) for a in (taps, lags, counts)))


def layout_kernel(acc_ref, out_ref, buf, sem):
    rows, slots = buf.shape[1], buf.shape[0]
    steps = 2048 // rows
    puts = []
    for s in range(2 * steps):
        lag, first = s // steps, (s % steps) * rows
        if s >= slots:
            puts[s - slots].wait()
        buf[s % slots] = jnp.swapaxes(acc_ref[lag, :, first:first + rows, :].astype(f32), 0, 1).astype(bf16)
        put = pltpu.make_async_copy(buf.at[s % slots], out_ref.at[lag, first:first + rows], sem.at[s % slots])
        put.start()
        puts.append(put)
    for put in puts[-slots:]:
        put.wait()


def laid_out(acc):
    rows, slots = 256, 4
    return pl.pallas_call(
        layout_kernel,
        out_shape=jax.ShapeDtypeStruct((2, 2048, 8, 128), bf16),
        in_specs=[pl.BlockSpec(memory_space=pltpu.VMEM)],
        out_specs=pl.BlockSpec(memory_space=pl.ANY),
        scratch_shapes=[pltpu.VMEM((slots, rows, 8, 128), bf16), pltpu.SemaphoreType.DMA((slots,))],
        compiler_params=pltpu.CompilerParams(vmem_limit_bytes=24 << 20),
        name="layout",
    )(acc)


def shards(spike_counts, kernel_taps, lag_bins):
    return laid_out(gathered(kernel_taps, lag_bins, spike_counts))


def solution(mesh):
    placed = (P(("row", "blk"), None), P(), P())
    return jax.shard_map(
        shards, mesh=mesh, in_specs=placed, out_specs=P(None, "row", None, "blk"), check_vma=False
    )
```

time: 83.1 us -> 62 us (0.75)
  Pallas kernels: 80.4 us -> 61.7 us
  local copies, waits for them, and re-layouts: 2.53 us -> 0 us
    pallas_call x1, Pallas kernels: 73.9 us -> 56.9 us  [gathered(): pl.pallas_call(gather_kernel, out_shape=jax.ShapeDtypeStruct((2, 8, 2048,...]
    unnamed x6 -> x0, local copies, waits for them, and re-layouts: 2.53 us -> none
    pallas_call x1, Pallas kernels: 6.49 us -> 4.77 us  [laid_out(): pl.pallas_call(layout_kernel, out_shape=jax.ShapeDtypeStruct((2, 2048, 8,...]
where the time goes in v2:
time: 62 us; the launch traced here: 61.9 us
  Pallas kernels  61.7 us (100%)
    pallas_call x1, Pallas kernels, gathered(): pl.pallas_call(gather_kernel, out_shape=jax.ShapeDtypeStruct((2, 8, 2048,...  56.9 us
    pallas_call x1, Pallas kernels, laid_out(): pl.pallas_call(layout_kernel, out_shape=jax.ShapeDtypeStruct((2, 2048, 8,...  4.77 us

profile of v2, /device:TPU:1, one launch (start us, length us, event | category | flops | bytes accessed | tf_op | source)
XLA Modules:
  0.0 61.9 jit_solution(12836492772227514692)
XLA Ops:
  0.0 56.9 %gather_products.1.acc_ref = bf16[2,8,2048,128]{3,2,1,0:T(8,128)(2,1)S(1)} custom-call(s32[16]{0:T(128)} %taps_hbm.1, s32[2]{0:T(128)} %lag_hbm.1, s32[128,2048]{1,0:T(8,128)} %counts_hbm.1), custom_call_target="tpu_custom_call" | custom-call | tf_op jit(solution)/shard_map/gather_products/pallas_call | solution.py:361
  56.9 4.8 %layout.1 = bf16[2,2048,8,128]{3,2,1,0:T(8,128)(2,1)} custom-call(bf16[2,8,2048,128]{3,2,1,0:T(8,128)(2,1)S(1)} %gather_products.1.acc_ref), custom_call_target="tpu_custom_call" | custom-call | tf_op jit(solution)/shard_map/layout/pallas_call | solution.py:412

commit v3 on v2

--- a/solution.py
+++ b/solution.py
@@ -28,7 +28,7 @@
 
 
 def gather_kernel(taps_hbm, lag_hbm, counts_hbm, acc_ref,
-                  taps_ref, lag_ref, counts, raw, bbuf, wz, ws, ft, fr, popt, popr, wrow, wcol, wsum,
+                  taps_ref, lag_ref, counts, raw, bbuf, wz, ws, via, ft, fr, popt, popr, wrow, wcol, wsum,
                   own_sum, part_sum, got1, got2, lsem, snd1, rcv1, snd2, rcv2, ssem, rsem):
     row = lax.axis_index("row")
     blk = lax.axis_index("blk")
@@ -105,17 +105,17 @@
         first = slot * 256 + other * ROWS + h * HALF
         return bbuf.at[first:first + HALF, :]
 
+    def bb_rows(slot, first, size):
+        return bbuf.at[slot * 256 + first:slot * 256 + first + size, :]
+
     for h in range(2):
         copy(("xp", h), raw_half(O, h), raw_half(XM, h), xp)
         copy(("xm", h), raw_half(O, h), raw_half(XP, h), xm)
         copy(("yp", h), raw_half(O, h), raw_half(YM, h), yp)
         copy(("ym", h), raw_half(O, h), raw_half(YP, h), ym)
-        copy(("pxp", h), wz_half(S_Z, h), wz_half(S_ZM, h), xp)
-        copy(("pxm", h), wz_half(S_Z, h), wz_half(S_ZP, h), xm)
         copy(("qyp", h), bb_half(S_Z, h), bb_half(S_ZM, h), yp)
         copy(("qym", h), bb_half(S_Z, h), bb_half(S_ZP, h), ym)
-        copy(("zy", h), bb_half(S_2, h), bb_half(S_Z2, h), zq)
-        for slot in (S_Z2, S_ZM, S_ZP):
+        for slot in (S_ZM, S_ZP):
             copy(("c", slot, h), bb_half(slot, h), bb_half(slot, h, 1), cp)
     for k in range(4):
         copy(("zq", k), raw_quarter(O, k), raw_quarter(QZ, k), zq)
@@ -124,8 +124,19 @@
     copy("x2m", raw_half(XP, 1), raw_half(X2, 1), xm)
     copy("y2p", raw_half(YM, 0), raw_half(Y2, 0), yp)
     copy("y2m", raw_half(YP, 1), raw_half(Y2, 1), ym)
-    copy("px2p", wz_half(S_ZM, 0), wz_half(S_Z2, 0), xp)
-    copy("px2m", wz_half(S_ZP, 1), wz_half(S_Z2, 1), xm)
+    copy("a1", wz_half(S_M, 0), via.at[0], zq)
+    copy("a2", via.at[0], wz_half(S_ZM, 0), zo)
+    copy("b1", wz_half(S_P, 1), via.at[1], zo)
+    copy("b2", via.at[1], wz_half(S_ZP, 1), zq)
+    copy("pxp", wz_half(S_Z, 1), wz_half(S_ZM, 1), xp)
+    copy("pxm", wz_half(S_Z, 0), wz_half(S_ZP, 0), xm)
+    copy("px2p", wz_half(S_ZM, 1), wz_half(S_Z2, 1), xp)
+    copy("px2m", wz_half(S_ZP, 0), wz_half(S_Z2, 0), xm)
+    copy("qy2p", bb_rows(S_ZM, 0, QUARTER), bb_rows(S_Z2, 0, QUARTER), yp)
+    copy("qy2m", bb_rows(S_ZP, 3 * QUARTER, QUARTER), bb_rows(S_Z2, 3 * QUARTER, QUARTER), ym)
+    copy("zy", bb_rows(S_2, QUARTER, HALF), bb_rows(S_Z2, QUARTER, HALF), zq)
+    for k, size in ((0, QUARTER), (QUARTER, HALF), (3 * QUARTER, QUARTER)):
+        copy(("c", S_Z2, k), bb_rows(S_Z2, k, size), bb_rows(S_Z2, ROWS + k, size), cp)
     for slot in (S_O, S_Z, S_M, S_P, S_2):
         copy(("c", slot), bbuf.at[slot * 256:slot * 256 + ROWS, :],
              bbuf.at[slot * 256 + ROWS:slot * 256 + 2 * ROWS, :], cp)
@@ -295,6 +306,7 @@
             return 0
         lax.fori_loop(0, count, one, 0)
 
+    near = (S_O, S_Z, S_M, S_P)
     to_rows(O, S_O)
     start(("c", S_O))
     arrived(("zq", 2))
@@ -304,48 +316,60 @@
     start(("zo", 3))
     to_rows(QZ, S_Z)
     start(("qyp", 0), ("qym", 1), ("qyp", 1), ("qym", 0), ("c", S_Z))
-    arrived(("xp", 1), ("xm", 0), ("yp", 1), ("ym", 0))
+    arrived(("xp", 1), ("xm", 0))
+    to_columns(XM, S_M)
+    start("a1")
+    to_columns(XP, S_P)
+    start("b1")
+    arrived(("yp", 1), ("ym", 0))
     to_rows(YM, S_M)
     start(("c", S_M))
+    arrived(("zo", 0), ("zo", 1), ("zo", 2), ("zo", 3))
+    to_columns(PZ, S_Z)
+    start("pxp", "pxm")
     to_rows(YP, S_P)
     start(("c", S_P))
-    to_columns(XM, S_M)
-    to_columns(XP, S_P)
-    arrived(("zo", 0), ("zo", 1), ("zo", 2), ("zo", 3))
-    to_columns(PZ, S_Z)
-    start(("pxp", 0), ("pxm", 1), ("pxp", 1), ("pxm", 0))
     arrived(("c", S_O), ("c", S_Z))
-    multiply_pairs(S_O, 2, 1, (S_O, S_Z, S_M, S_P))
+    multiply_pairs(S_O, 2, 1, near)
     arrived("y2p", "y2m")
     to_rows(Y2, S_2)
-    start(("zy", 0), ("zy", 1), ("c", S_2))
+    start(("c", S_2))
+    arrived("a1", "b1")
+    start("a2", "b2", "zy")
     arrived("x2p", "x2m")
     to_columns(X2, S_2)
-    arrived(("c", S_M), ("c", S_P), ("c", S_2))
-    multiply_pairs(S_M, 3, 1, (S_O, S_Z, S_M, S_P))
+    arrived(("c", S_M), ("c", S_P))
+    multiply_pairs(S_M, 2, 1, near)
+    arrived(("qyp", 0), ("qym", 1))
+    start("qy2p", "qy2m", ("c", S_ZM, 0), ("c", S_ZP, 1))
+    arrived("pxp", "pxm")
+    start("px2p", "px2m")
+    arrived(("c", S_2))
+    multiply(whole(S_2), near)
     multiply(whole(S_O, 5), (S_2,))
-    arrived(("qyp", 0), ("qym", 1))
-    start(("c", S_ZM, 0), ("c", S_ZP, 1))
-    arrived(("pxp", 0), ("pxm", 1))
-    start("px2p", "px2m")
     arrived(("c", S_ZM, 0), ("c", S_ZP, 1))
-    multiply(halves(S_ZM, 0) + halves(S_ZP, 1), (S_O, S_Z, S_M, S_P, S_2))
+    early = halves(S_ZM, 0) + halves(S_ZP, 1)
+    later = halves(S_ZM, 1) + halves(S_ZP, 0)
+    multiply(early, near + (S_2,))
+    arrived("a2")
+    move(S_ZM)
+    multiply(whole(S_O, 5) + early, (S_ZM,))
     arrived(("qyp", 1), ("qym", 0))
     start(("c", S_ZM, 1), ("c", S_ZP, 0))
-    arrived(("pxp", 1), ("pxm", 0))
-    move(S_ZM)
-    move(S_ZP)
-    multiply_pairs(S_O, 2, 2, (S_ZM, S_ZP))
-    arrived(("zy", 0), ("zy", 1))
-    start(("c", S_Z2, 0), ("c", S_Z2, 1))
-    arrived(("c", S_ZM, 1), ("c", S_ZP, 0))
-    multiply(halves(S_ZM, 1) + halves(S_ZP, 0), (S_O, S_Z, S_M, S_P, S_2))
-    multiply(whole(S_2) + whole(S_ZM, 2), (S_ZM, S_ZP))
-    arrived(("c", S_Z2, 0), ("c", S_Z2, 1))
-    multiply(whole(S_Z2), (S_O, S_Z, S_M, S_P, S_2, S_ZM, S_ZP))
     arrived("px2p", "px2m")
     move(S_Z2)
-    multiply_pairs(S_O, 2, 4, (S_Z2,))
+    multiply(whole(S_O, 5) + early, (S_Z2,))
+    arrived("qy2p", "qy2m")
+    start(("c", S_Z2, 0), ("c", S_Z2, 3 * QUARTER))
+    arrived(("c", S_ZM, 1), ("c", S_ZP, 0))
+    multiply(later, near + (S_2, S_ZM, S_Z2))
+    arrived("b2")
+    move(S_ZP)
+    arrived("zy")
+    start(("c", S_Z2, QUARTER))
+    multiply(whole(S_O, 5) + whole(S_ZM, 2), (S_ZP,))
+    arrived(("c", S_Z2, 0), ("c", S_Z2, QUARTER), ("c", S_Z2, 3 * QUARTER))
+    multiply(whole(S_Z2), near + (S_2, S_ZM, S_Z2, S_ZP))
 
     for s in step1 + step2:
         s.wait_send()
@@ -353,7 +377,7 @@
         copies[name].wait_send()
 
 
-N_COPIES = 2 * 12 + 8 + 6 + 5
+N_COPIES = 2 * 8 + 8 + 4 + 8 + 3 + 3 + 5
 
 
 def gathered(taps, lags, counts):
@@ -371,6 +395,7 @@
             pltpu.VMEM((2048, BINS), bf16),
             pltpu.VMEM((8, BINS + LAGMAX, 128), bf16),
             pltpu.VMEM((8, BINS, 128), bf16),
+            pltpu.VMEM((2, BINS // 2, 128), bf16),
             pltpu.VMEM((BINS + LAGMAX, 128), f32),
             pltpu.VMEM((ROWS, BINS), f32),
             pltpu.VMEM((BINS, 128), f32),

time: 62 us -> 67 us (1.081)
  Pallas kernels: 61.7 us -> 66.7 us
    pallas_call x1, Pallas kernels: 56.9 us -> 62 us  [gathered(): pl.pallas_call(gather_kernel, out_shape=jax.ShapeDtypeStruct((2, 8, 2048,...]
where the time goes in v3:
time: 67 us; the launch traced here: 66.9 us
  Pallas kernels  66.7 us (100%)
    pallas_call x1, Pallas kernels, gathered(): pl.pallas_call(gather_kernel, out_shape=jax.ShapeDtypeStruct((2, 8, 2048,...  62 us
    pallas_call x1, Pallas kernels, laid_out(): pl.pallas_call(layout_kernel, out_shape=jax.ShapeDtypeStruct((2, 2048, 8,...  4.77 us

profile of v3, /device:TPU:1, one launch (start us, length us, event | category | flops | bytes accessed | tf_op | source)
XLA Modules:
  0.0 66.9 jit_solution(18235449096350317294)
XLA Ops:
  0.0 62.0 %gather_products.1.acc_ref = bf16[2,8,2048,128]{3,2,1,0:T(8,128)(2,1)S(1)} custom-call(s32[16]{0:T(128)} %taps_hbm.1, s32[2]{0:T(128)} %lag_hbm.1, s32[128,2048]{1,0:T(8,128)} %counts_hbm.1), custom_call_target="tpu_custom_call" | custom-call | tf_op jit(solution)/shard_map/gather_products/pallas_call | solution.py:385
  62.0 4.8 %layout.1 = bf16[2,2048,8,128]{3,2,1,0:T(8,128)(2,1)} custom-call(bf16[2,8,2048,128]{3,2,1,0:T(8,128)(2,1)S(1)} %gather_products.1.acc_ref), custom_call_target="tpu_custom_call" | custom-call | tf_op jit(solution)/shard_map/layout/pallas_call | solution.py:437

commit v4 on v2

--- a/solution.py
+++ b/solution.py
@@ -173,6 +173,8 @@
     start("y2p", "y2m")
     arrived(("zq", 1))
     start(("zo", 1))
+    arrived(("zq", 2))
+    start(("zo", 2))
 
     for s in step2:
         s.wait_recv()
@@ -295,54 +297,55 @@
             return 0
         lax.fori_loop(0, count, one, 0)
 
+    near = (S_O, S_Z, S_M, S_P)
     to_rows(O, S_O)
     start(("c", S_O))
-    arrived(("zq", 2))
-    start(("zo", 2))
-    to_columns(O, S_O)
     arrived(("zq", 3))
     start(("zo", 3))
     to_rows(QZ, S_Z)
     start(("qyp", 0), ("qym", 1), ("qyp", 1), ("qym", 0), ("c", S_Z))
+    to_columns(O, S_O)
     arrived(("xp", 1), ("xm", 0), ("yp", 1), ("ym", 0))
+    to_columns(XM, S_M)
+    to_columns(XP, S_P)
     to_rows(YM, S_M)
     start(("c", S_M))
-    to_rows(YP, S_P)
-    start(("c", S_P))
-    to_columns(XM, S_M)
-    to_columns(XP, S_P)
     arrived(("zo", 0), ("zo", 1), ("zo", 2), ("zo", 3))
     to_columns(PZ, S_Z)
     start(("pxp", 0), ("pxm", 1), ("pxp", 1), ("pxm", 0))
-    arrived(("c", S_O), ("c", S_Z))
-    multiply_pairs(S_O, 2, 1, (S_O, S_Z, S_M, S_P))
+    to_rows(YP, S_P)
+    start(("c", S_P))
     arrived("y2p", "y2m")
     to_rows(Y2, S_2)
     start(("zy", 0), ("zy", 1), ("c", S_2))
+    arrived(("c", S_O), ("c", S_Z))
+    multiply_pairs(S_O, 2, 1, near)
     arrived("x2p", "x2m")
     to_columns(X2, S_2)
     arrived(("c", S_M), ("c", S_P), ("c", S_2))
-    multiply_pairs(S_M, 3, 1, (S_O, S_Z, S_M, S_P))
-    multiply(whole(S_O, 5), (S_2,))
+    multiply_pairs(S_M, 3, 1, near)
     arrived(("qyp", 0), ("qym", 1))
     start(("c", S_ZM, 0), ("c", S_ZP, 1))
     arrived(("pxp", 0), ("pxm", 1))
     start("px2p", "px2m")
+    multiply(whole(S_O, 5), (S_2,))
+    early = halves(S_ZM, 0) + halves(S_ZP, 1)
+    later = halves(S_ZM, 1) + halves(S_ZP, 0)
     arrived(("c", S_ZM, 0), ("c", S_ZP, 1))
-    multiply(halves(S_ZM, 0) + halves(S_ZP, 1), (S_O, S_Z, S_M, S_P, S_2))
+    multiply(early, near + (S_2,))
     arrived(("qyp", 1), ("qym", 0))
     start(("c", S_ZM, 1), ("c", S_ZP, 0))
     arrived(("pxp", 1), ("pxm", 0))
     move(S_ZM)
     move(S_ZP)
     multiply_pairs(S_O, 2, 2, (S_ZM, S_ZP))
+    multiply(whole(S_2) + early, (S_ZM, S_ZP))
     arrived(("zy", 0), ("zy", 1))
     start(("c", S_Z2, 0), ("c", S_Z2, 1))
     arrived(("c", S_ZM, 1), ("c", S_ZP, 0))
-    multiply(halves(S_ZM, 1) + halves(S_ZP, 0), (S_O, S_Z, S_M, S_P, S_2))
-    multiply(whole(S_2) + whole(S_ZM, 2), (S_ZM, S_ZP))
+    multiply(later, near + (S_2, S_ZM, S_ZP))
     arrived(("c", S_Z2, 0), ("c", S_Z2, 1))
-    multiply(whole(S_Z2), (S_O, S_Z, S_M, S_P, S_2, S_ZM, S_ZP))
+    multiply(whole(S_Z2), near + (S_2, S_ZM, S_ZP))
     arrived("px2p", "px2m")
     move(S_Z2)
     multiply_pairs(S_O, 2, 4, (S_Z2,))

time: 62 us -> 61.7 us (level)
  no operation moved by 1% of the time
where the time goes in v4:
time: 61.7 us; the launch traced here: 61.6 us
  Pallas kernels  61.4 us (100%)
    pallas_call x1, Pallas kernels, gathered(): pl.pallas_call(gather_kernel, out_shape=jax.ShapeDtypeStruct((2, 8, 2048,...  56.7 us
    pallas_call x1, Pallas kernels, laid_out(): pl.pallas_call(layout_kernel, out_shape=jax.ShapeDtypeStruct((2, 2048, 8,...  4.77 us

profile of v4, /device:TPU:1, one launch (start us, length us, event | category | flops | bytes accessed | tf_op | source)
XLA Modules:
  0.0 61.6 jit_solution(4115387581322032184)
XLA Ops:
  0.0 56.7 %gather_products.1.acc_ref = bf16[2,8,2048,128]{3,2,1,0:T(8,128)(2,1)S(1)} custom-call(s32[16]{0:T(128)} %taps_hbm.1, s32[2]{0:T(128)} %lag_hbm.1, s32[128,2048]{1,0:T(8,128)} %counts_hbm.1), custom_call_target="tpu_custom_call" | custom-call | tf_op jit(solution)/shard_map/gather_products/pallas_call | solution.py:364
  56.7 4.8 %layout.1 = bf16[2,2048,8,128]{3,2,1,0:T(8,128)(2,1)} custom-call(bf16[2,8,2048,128]{3,2,1,0:T(8,128)(2,1)S(1)} %gather_products.1.acc_ref), custom_call_target="tpu_custom_call" | custom-call | tf_op jit(solution)/shard_map/layout/pallas_call | solution.py:415

commit v5 on v3

--- a/solution.py
+++ b/solution.py
@@ -184,6 +184,8 @@
     start("y2p", "y2m")
     arrived(("zq", 1))
     start(("zo", 1))
+    arrived(("zq", 2))
+    start(("zo", 2))
 
     for s in step2:
         s.wait_recv()
@@ -307,11 +309,10 @@
         lax.fori_loop(0, count, one, 0)
 
     near = (S_O, S_Z, S_M, S_P)
+    early = halves(S_ZM, 0) + halves(S_ZP, 1)
+    later = halves(S_ZM, 1) + halves(S_ZP, 0)
     to_rows(O, S_O)
     start(("c", S_O))
-    arrived(("zq", 2))
-    start(("zo", 2))
-    to_columns(O, S_O)
     arrived(("zq", 3))
     start(("zo", 3))
     to_rows(QZ, S_Z)
@@ -321,6 +322,7 @@
     start("a1")
     to_columns(XP, S_P)
     start("b1")
+    to_columns(O, S_O)
     arrived(("yp", 1), ("ym", 0))
     to_rows(YM, S_M)
     start(("c", S_M))
@@ -329,15 +331,15 @@
     start("pxp", "pxm")
     to_rows(YP, S_P)
     start(("c", S_P))
+    arrived("y2p", "y2m")
+    to_rows(Y2, S_2)
+    start("zy", ("c", S_2))
     arrived(("c", S_O), ("c", S_Z))
     multiply_pairs(S_O, 2, 1, near)
-    arrived("y2p", "y2m")
-    to_rows(Y2, S_2)
-    start(("c", S_2))
-    arrived("a1", "b1")
-    start("a2", "b2", "zy")
     arrived("x2p", "x2m")
     to_columns(X2, S_2)
+    arrived("a1", "b1")
+    start("a2", "b2")
     arrived(("c", S_M), ("c", S_P))
     multiply_pairs(S_M, 2, 1, near)
     arrived(("qyp", 0), ("qym", 1))
@@ -348,8 +350,6 @@
     multiply(whole(S_2), near)
     multiply(whole(S_O, 5), (S_2,))
     arrived(("c", S_ZM, 0), ("c", S_ZP, 1))
-    early = halves(S_ZM, 0) + halves(S_ZP, 1)
-    later = halves(S_ZM, 1) + halves(S_ZP, 0)
     multiply(early, near + (S_2,))
     arrived("a2")
     move(S_ZM)
@@ -359,17 +359,14 @@
     arrived("px2p", "px2m")
     move(S_Z2)
     multiply(whole(S_O, 5) + early, (S_Z2,))
-    arrived("qy2p", "qy2m")
-    start(("c", S_Z2, 0), ("c", S_Z2, 3 * QUARTER))
-    arrived(("c", S_ZM, 1), ("c", S_ZP, 0))
-    multiply(later, near + (S_2, S_ZM, S_Z2))
+    arrived("qy2p", "qy2m", "zy")
+    start(("c", S_Z2, 0), ("c", S_Z2, 3 * QUARTER), ("c", S_Z2, QUARTER))
     arrived("b2")
     move(S_ZP)
-    arrived("zy")
-    start(("c", S_Z2, QUARTER))
-    multiply(whole(S_O, 5) + whole(S_ZM, 2), (S_ZP,))
+    multiply(whole(S_O, 5) + early, (S_ZP,))
+    arrived(("c", S_ZM, 1), ("c", S_ZP, 0))
     arrived(("c", S_Z2, 0), ("c", S_Z2, QUARTER), ("c", S_Z2, 3 * QUARTER))
-    multiply(whole(S_Z2), near + (S_2, S_ZM, S_Z2, S_ZP))
+    multiply(later + whole(S_Z2), near + (S_2, S_ZM, S_Z2, S_ZP))
 
     for s in step1 + step2:
         s.wait_send()

time: 67 us -> 65.3 us (0.975)
  Pallas kernels: 66.7 us -> 64.5 us
    pallas_call x1, Pallas kernels: 62 us -> 59.7 us  [gathered(): pl.pallas_call(gather_kernel, out_shape=jax.ShapeDtypeStruct((2, 8, 2048,...]
where the time goes in v5:
time: 65.3 us; the launch traced here: 64.7 us
  Pallas kernels  64.5 us (99%)
    pallas_call x1, Pallas kernels, gathered(): pl.pallas_call(gather_kernel, out_shape=jax.ShapeDtypeStruct((2, 8, 2048,...  59.7 us
    pallas_call x1, Pallas kernels, laid_out(): pl.pallas_call(layout_kernel, out_shape=jax.ShapeDtypeStruct((2, 2048, 8,...  4.77 us

profile of v5, /device:TPU:1, one launch (start us, length us, event | category | flops | bytes accessed | tf_op | source)
XLA Modules:
  0.0 64.7 jit_solution(14706704719594129998)
XLA Ops:
  0.0 59.7 %gather_products.1.acc_ref = bf16[2,8,2048,128]{3,2,1,0:T(8,128)(2,1)S(1)} custom-call(s32[16]{0:T(128)} %taps_hbm.1, s32[2]{0:T(128)} %lag_hbm.1, s32[128,2048]{1,0:T(8,128)} %counts_hbm.1), custom_call_target="tpu_custom_call" | custom-call | tf_op jit(solution)/shard_map/gather_products/pallas_call | solution.py:382
  59.7 4.8 %layout.1 = bf16[2,2048,8,128]{3,2,1,0:T(8,128)(2,1)} custom-call(bf16[2,8,2048,128]{3,2,1,0:T(8,128)(2,1)S(1)} %gather_products.1.acc_ref), custom_call_target="tpu_custom_call" | custom-call | tf_op jit(solution)/shard_map/layout/pallas_call | solution.py:434

commit v6 on v4

--- a/solution.py
+++ b/solution.py
@@ -338,17 +338,16 @@
     arrived(("pxp", 1), ("pxm", 0))
     move(S_ZM)
     move(S_ZP)
-    multiply_pairs(S_O, 2, 2, (S_ZM, S_ZP))
-    multiply(whole(S_2) + early, (S_ZM, S_ZP))
+    multiply(whole(S_O, 4), (S_ZM, S_ZP))
     arrived(("zy", 0), ("zy", 1))
     start(("c", S_Z2, 0), ("c", S_Z2, 1))
+    multiply(whole(S_2) + early, (S_ZM, S_ZP))
     arrived(("c", S_ZM, 1), ("c", S_ZP, 0))
-    multiply(later, near + (S_2, S_ZM, S_ZP))
     arrived(("c", S_Z2, 0), ("c", S_Z2, 1))
-    multiply(whole(S_Z2), near + (S_2, S_ZM, S_ZP))
+    multiply(later + whole(S_Z2), near + (S_2, S_ZM, S_ZP))
     arrived("px2p", "px2m")
     move(S_Z2)
-    multiply_pairs(S_O, 2, 4, (S_Z2,))
+    multiply(whole(S_O, 8), (S_Z2,))
 
     for s in step1 + step2:
         s.wait_send()
@@ -402,7 +401,7 @@
         lag, first = s // steps, (s % steps) * rows
         if s >= slots:
             puts[s - slots].wait()
-        buf[s % slots] = jnp.swapaxes(acc_ref[lag, :, first:first + rows, :].astype(f32), 0, 1).astype(bf16)
+        buf[s % slots] = jnp.swapaxes(acc_ref[lag, :, first:first + rows, :], 0, 1)
         put = pltpu.make_async_copy(buf.at[s % slots], out_ref.at[lag, first:first + rows], sem.at[s % slots])
         put.start()
         puts.append(put)
@@ -411,7 +410,7 @@
 
 
 def laid_out(acc):
-    rows, slots = 256, 4
+    rows, slots = 256, 8
     return pl.pallas_call(
         layout_kernel,
         out_shape=jax.ShapeDtypeStruct((2, 2048, 8, 128), bf16),

time: 61.7 us -> 61.8 us (level)
    pallas_call x1, Pallas kernels: 56.7 us -> 58 us  [gathered(): pl.pallas_call(gather_kernel, out_shape=jax.ShapeDtypeStruct((2, 8, 2048,...]
    pallas_call x1, Pallas kernels: 4.77 us -> 3.51 us  [laid_out(): pl.pallas_call(layout_kernel, out_shape=jax.ShapeDtypeStruct((2, 2048, 8,...]
where the time goes in v6:
time: 61.8 us; the launch traced here: 61.6 us
  Pallas kernels  61.5 us (100%)
    pallas_call x1, Pallas kernels, gathered(): pl.pallas_call(gather_kernel, out_shape=jax.ShapeDtypeStruct((2, 8, 2048,...  58 us
    pallas_call x1, Pallas kernels, laid_out(): pl.pallas_call(layout_kernel, out_shape=jax.ShapeDtypeStruct((2, 2048, 8,...  3.51 us

profile of v6, /device:TPU:1, one launch (start us, length us, event | category | flops | bytes accessed | tf_op | source)
XLA Modules:
  0.0 61.6 jit_solution(2656465999348530248)
XLA Ops:
  0.0 58.0 %gather_products.1.acc_ref = bf16[2,8,2048,128]{3,2,1,0:T(8,128)(2,1)S(1)} custom-call(s32[16]{0:T(128)} %taps_hbm.1, s32[2]{0:T(128)} %lag_hbm.1, s32[128,2048]{1,0:T(8,128)} %counts_hbm.1), custom_call_target="tpu_custom_call" | custom-call | tf_op jit(solution)/shard_map/gather_products/pallas_call | solution.py:363
  58.0 3.5 %layout.1 = bf16[2,2048,8,128]{3,2,1,0:T(8,128)(2,1)} custom-call(bf16[2,8,2048,128]{3,2,1,0:T(8,128)(2,1)S(1)} %gather_products.1.acc_ref), custom_call_target="tpu_custom_call" | custom-call | tf_op jit(solution)/shard_map/layout/pallas_call | solution.py:414

commit v7 on v4

--- a/solution.py
+++ b/solution.py
@@ -402,7 +402,7 @@
         lag, first = s // steps, (s % steps) * rows
         if s >= slots:
             puts[s - slots].wait()
-        buf[s % slots] = jnp.swapaxes(acc_ref[lag, :, first:first + rows, :].astype(f32), 0, 1).astype(bf16)
+        buf[s % slots] = jnp.swapaxes(acc_ref[lag, :, first:first + rows, :], 0, 1)
         put = pltpu.make_async_copy(buf.at[s % slots], out_ref.at[lag, first:first + rows], sem.at[s % slots])
         put.start()
         puts.append(put)
@@ -411,7 +411,7 @@
 
 
 def laid_out(acc):
-    rows, slots = 256, 4
+    rows, slots = 256, 8
     return pl.pallas_call(
         layout_kernel,
         out_shape=jax.ShapeDtypeStruct((2, 2048, 8, 128), bf16),

time: 61.7 us -> 60.5 us (0.981)
  Pallas kernels: 61.4 us -> 60.2 us
    pallas_call x1, Pallas kernels: 4.77 us -> 3.51 us  [laid_out(): pl.pallas_call(layout_kernel, out_shape=jax.ShapeDtypeStruct((2, 2048, 8,...]
where the time goes in v7:
time: 60.5 us; the launch traced here: 60.4 us
  Pallas kernels  60.2 us (100%)
    pallas_call x1, Pallas kernels, gathered(): pl.pallas_call(gather_kernel, out_shape=jax.ShapeDtypeStruct((2, 8, 2048,...  56.7 us
    pallas_call x1, Pallas kernels, laid_out(): pl.pallas_call(layout_kernel, out_shape=jax.ShapeDtypeStruct((2, 2048, 8,...  3.51 us

profile of v7, /device:TPU:1, one launch (start us, length us, event | category | flops | bytes accessed | tf_op | source)
XLA Modules:
  0.0 60.4 jit_solution(12390693399976492414)
XLA Ops:
  0.0 56.7 %gather_products.1.acc_ref = bf16[2,8,2048,128]{3,2,1,0:T(8,128)(2,1)S(1)} custom-call(s32[16]{0:T(128)} %taps_hbm.1, s32[2]{0:T(128)} %lag_hbm.1, s32[128,2048]{1,0:T(8,128)} %counts_hbm.1), custom_call_target="tpu_custom_call" | custom-call | tf_op jit(solution)/shard_map/gather_products/pallas_call | solution.py:364
  56.7 3.5 %layout.1 = bf16[2,2048,8,128]{3,2,1,0:T(8,128)(2,1)} custom-call(bf16[2,8,2048,128]{3,2,1,0:T(8,128)(2,1)S(1)} %gather_products.1.acc_ref), custom_call_target="tpu_custom_call" | custom-call | tf_op jit(solution)/shard_map/layout/pallas_call | solution.py:415

commit v8 on v7

--- a/solution.py
+++ b/solution.py
@@ -348,7 +348,7 @@
     multiply(whole(S_Z2), near + (S_2, S_ZM, S_ZP))
     arrived("px2p", "px2m")
     move(S_Z2)
-    multiply_pairs(S_O, 2, 4, (S_Z2,))
+    multiply(whole(S_O, 8), (S_Z2,))
 
     for s in step1 + step2:
         s.wait_send()

time: 60.5 us -> 60.4 us (level)
  no operation moved by 1% of the time
where the time goes in v8:
time: 60.4 us; the launch traced here: 60.3 us
  Pallas kernels  60.1 us (100%)
    pallas_call x1, Pallas kernels, gathered(): pl.pallas_call(gather_kernel, out_shape=jax.ShapeDtypeStruct((2, 8, 2048,...  56.6 us
    pallas_call x1, Pallas kernels, laid_out(): pl.pallas_call(layout_kernel, out_shape=jax.ShapeDtypeStruct((2, 2048, 8,...  3.51 us

profile of v8, /device:TPU:1, one launch (start us, length us, event | category | flops | bytes accessed | tf_op | source)
XLA Modules:
  0.0 60.3 jit_solution(15258213373741877788)
XLA Ops:
  0.0 56.6 %gather_products.1.acc_ref = bf16[2,8,2048,128]{3,2,1,0:T(8,128)(2,1)S(1)} custom-call(s32[16]{0:T(128)} %taps_hbm.1, s32[2]{0:T(128)} %lag_hbm.1, s32[128,2048]{1,0:T(8,128)} %counts_hbm.1), custom_call_target="tpu_custom_call" | custom-call | tf_op jit(solution)/shard_map/gather_products/pallas_call | solution.py:364
  56.6 3.5 %layout.1 = bf16[2,2048,8,128]{3,2,1,0:T(8,128)(2,1)} custom-call(bf16[2,8,2048,128]{3,2,1,0:T(8,128)(2,1)S(1)} %gather_products.1.acc_ref), custom_call_target="tpu_custom_call" | custom-call | tf_op jit(solution)/shard_map/layout/pallas_call | solution.py:415
